TPU v7x, 32 devices: a whole 2x2x4 slice. The times are simulated.
32 devices in a mesh: rows: 8 (over z, x), scales: 4 (over y, core).
Axes of the slice: x: 2, y: 2, z: 4, core: 2. Of those that a mesh axis runs over, the one named last changes fastest.
Arguments:
- image_now: float32 [256, 8192], P(('rows', 'scales')), may hold values from 0.1 to 4
- gradient: float32 [256, 8192], P(('rows', 'scales')), may hold values from -140 to 140
- hessian_weight: float32 [256, 8192], P(('rows', 'scales')), may hold values from 0.1 to 10
- psf_tiles: float32 [32, 256], P(('rows', 'scales')), may hold values from -0.5 to 1.7
- facet_of_row: int32 [256], P(('rows', 'scales')), may hold values from 0 to 31, never falling along the last dimension, each value on 1 to 32 neighbouring positions
- tile_slot: int32 [32], replicated, may hold values from 0 to 31, each once
- thresholds: float32 [4], replicated, may hold values from 0.2 to 2
Outputs:
- new_image: float32 [256, 8192], P(('rows', 'scales'))
Inputs may be any that keep to these rules, and one draw needn't show every extreme that they name: `facet_of_row`: facet numbers never fall along the rows; every facet covers 1 to 32 rows, and some facet exactly 32. `tile_slot`: each facet's tile stands in a different row of psf_tiles, and every row holds one.
All inputs are finite; a program needn't handle non-finite values.
Results may differ from a plain program's by a relative error of at most 0.0001.
Values sent between devices are 32-bit elements; how exact they have to be, the bound alone decides.
A program may use at most 64 MiB of HBM per device.

v0:
```python
import jax
import jax.numpy as jnp
from jax import lax
from jax.sharding import PartitionSpec as P

TILE = 16
SUBITERS = 2
SPLINE_EDGE = 0.0625
SPLINE_NEAR = 0.25
SPLINE_MID = 0.375


def padded_2(cells, sides, width):
    for axis, dim in sides:
        count = lax.axis_size(axis)
        ends = count - 1
        head = lax.slice_in_dim(cells, 0, width, axis=dim)
        tail = lax.slice_in_dim(cells, cells.shape[dim] - width, cells.shape[dim], axis=dim)
        cells = jnp.concatenate(
            [
                lax.ppermute(tail, axis, [(i, (i + 1) % count) for i in range(ends)]),
                cells,
                lax.ppermute(head, axis, [((i + 1) % count, i) for i in range(ends)]),
            ],
            axis=dim,
        )
    return cells


def along_columns(source, spacing):
    length = source.shape[1]
    padded = jnp.pad(source, ((0, 0), (2 * spacing, 2 * spacing)))
    outer_pair = padded[:, 0:length] + padded[:, 4 * spacing : 4 * spacing + length]
    inner_pair = (
        padded[:, spacing : spacing + length] + padded[:, 3 * spacing : 3 * spacing + length]
    )
    return SPLINE_EDGE * outer_pair + SPLINE_NEAR * inner_pair + SPLINE_MID * source


def rows_traced(source, spacing, reach):
    length = source.shape[0]
    padded = jnp.pad(source, ((reach, reach), (0, 0)))

    def shifted_rows(offset):
        return lax.dynamic_slice_in_dim(padded, reach + offset, length, 0)

    outer_pair = shifted_rows(-2 * spacing) + shifted_rows(2 * spacing)
    inner_pair = shifted_rows(-spacing) + shifted_rows(spacing)
    return SPLINE_EDGE * outer_pair + SPLINE_NEAR * inner_pair + SPLINE_MID * source


def widen_band(source):
    half_tile = TILE // 2
    extended = padded_2(source, ((("rows", "scales"), 0),), half_tile)
    return jnp.pad(extended, ((0, 0), (half_tile, half_tile)))


def forward_blur(source, weights):
    band_rows, columns = source.shape
    padded = widen_band(source)

    def forward_add_tap_row(tap_row, summed):
        shifted = lax.dynamic_slice_in_dim(padded, tap_row, band_rows, 0)
        tap_weights = lax.dynamic_index_in_dim(weights, tap_row, 1, keepdims=False)
        for column in range(TILE):
            summed = (
                summed + tap_weights[:, column : column + 1] * shifted[:, column : column + columns]
            )
        return summed

    return lax.fori_loop(0, TILE, forward_add_tap_row, jnp.zeros((band_rows, columns), jnp.float32))


def adjoint_blur(source, wide_weights):
    band_rows, columns = source.shape
    half_tile = TILE // 2
    padded = widen_band(source)

    def adjoint_add_tap_row(tap_row, summed):
        offset = 2 * half_tile - tap_row
        shifted = lax.dynamic_slice_in_dim(padded, offset, band_rows, 0)
        weight_rows = lax.dynamic_slice_in_dim(wide_weights, offset, band_rows, 0)
        tap_weights = lax.dynamic_index_in_dim(weight_rows, tap_row, 1, keepdims=False)
        for column in range(TILE):
            offset_col = 2 * half_tile - column
            summed = (
                summed
                + tap_weights[:, column : column + 1]
                * shifted[:, offset_col : offset_col + columns]
            )
        return summed

    return lax.fori_loop(0, TILE, adjoint_add_tap_row, jnp.zeros((band_rows, columns), jnp.float32))


def body(image_now, gradient, hessian_weight, psf_tiles, facet_of_row, tile_slot, thresholds):
    band_rows, columns = image_now.shape
    half_tile = TILE // 2
    scale_count = lax.axis_size("scales")
    scale_index = lax.axis_index("scales")
    facet_ids = jnp.arange(tile_slot.shape[0], dtype=jnp.int32)
    slot_rows = jnp.sum(
        jnp.where(facet_of_row[:, None] == facet_ids[None, :], tile_slot[None, :], 0), axis=1
    )
    tiles_in = lax.all_gather(psf_tiles, ("rows", "scales"), axis=0, tiled=True)
    length = tiles_in.shape[0]
    onehot = (slot_rows[:, None] == jnp.arange(length, dtype=jnp.int32)[None, :]).astype(
        jnp.float32
    )
    flat_rows = jnp.dot(
        onehot, tiles_in, precision=lax.Precision.HIGHEST, preferred_element_type=jnp.float32
    )
    wide_rows = padded_2(flat_rows, ((("rows", "scales"), 0),), half_tile)
    weights = flat_rows.reshape(band_rows, TILE, TILE)
    wide_weights = wide_rows.reshape(band_rows + 2 * half_tile, TILE, TILE)
    level_gain = jnp.sum(jnp.where(jnp.arange(scale_count) == scale_index, thresholds, 0.0))
    reach = 2**scale_count

    def column_level(depth, plane):
        return rows_traced(plane, jnp.left_shift(jnp.int32(1), depth), reach)

    current = image_now
    for sweep in range(SUBITERS):
        change = current - image_now
        pushed = hessian_weight * forward_blur(change, weights)
        descent = gradient + adjoint_blur(pushed, wide_weights)
        blurred = forward_blur(descent, weights)
        totals = lax.psum(
            (jnp.sum(descent * descent), jnp.sum(hessian_weight * blurred * blurred)),
            ("rows", "scales"),
        )
        step_size = totals[0] / totals[1]
        trial = current - step_size * descent
        stripe = lax.all_gather(trial, "scales", axis=0, tiled=True)
        smooth = stripe
        lower = jnp.zeros_like(stripe)
        upper = jnp.zeros_like(stripe)
        for depth in range(scale_count):
            smoother = along_columns(smooth, 2**depth)
            lower = jnp.where(scale_index == depth, smooth, lower)
            upper = jnp.where(scale_index == depth, smoother, upper)
            smooth = smoother
        limit = step_size * level_gain
        lower_cols, upper_cols = (
            lax.all_to_all(lower, "rows", split_axis=1, concat_axis=0, tiled=True),
            lax.all_to_all(upper, "rows", split_axis=1, concat_axis=0, tiled=True),
        )
        lower_cols = lax.fori_loop(0, scale_index, column_level, lower_cols)
        upper_cols = lax.fori_loop(0, scale_index + 1, column_level, upper_cols)
        detail = lower_cols - upper_cols
        kept = (
            detail
            - jnp.clip(detail, -limit, limit)
            + jnp.where(scale_index == scale_count - 1, upper_cols, 0.0)
        )
        contribution = lax.all_to_all(kept, "rows", split_axis=0, concat_axis=1, tiled=True)
        current = lax.psum_scatter(contribution, "scales", scatter_dimension=0, tiled=True)
    return current


def solution(mesh):
    in_specs = (
        P(("rows", "scales"), None),
        P(("rows", "scales"), None),
        P(("rows", "scales"), None),
        P(("rows", "scales"), None),
        P(("rows", "scales")),
        P(),
        P(),
    )
    out_specs = P(("rows", "scales"), None)
    return jax.shard_map(body, mesh=mesh, in_specs=in_specs, out_specs=out_specs, check_vma=False)
```

profile of v0, /device:TPU:0, one launch (start us, length us, event | category | flops | bytes accessed | tf_op | source)
XLA Modules:
  0.0 672.7 jit_solution(16924233468898300590)
XLA Ops:
  7.6 2.4 collective-permute-start.2
  12.2 45.4 %all-gather = f32[32,1,256]{2,1,0:T(1,128)S(1)} all-gather(f32[1,1,256]{2,1,0:T(1,128)} %bitcast.79), channel_id=1, replica_groups=mesh['rows'=8,'scales'=4] {'rows','scales'}, dimensions={0}, use_global_device_ids=true | all-gather | bytes 33792 | tf_op jit(solution)/shard_map/all_gather | solution.py:105
  58.2 27.8 %while.146 = (s32[]{:T(128)}, f32[8,8192]{1,0:T(8,128)S(1)}, f32[8,16,16]{2,0,1:T(8,128)S(1)}, f32[24,8208]{1,0:T(8,128)S(1)}, s32[]{:T(128)}, /*index=5*/s32[]{...) while((s32[]{:T(128)}, f32[8,8192]{1,0:T(8,128)S(1)}, ...), condition=%wide.region_2.3_spmd.clone, body=%wide.region_1.2_spmd.clone.sunk | while | flops 2162706 | bytes 4721599 | solution.py:71
  86.1 2.3 collective-permute-start.4
  89.7 3.0 collective-permute-start
  94.0 2.5 collective-permute-done.1
  97.0 29.6 %while.147 = (s32[]{:T(128)}, f32[8,8192]{1,0:T(8,128)S(1)}, f32[24,16,16]{2,0,1:T(8,128)S(1)}, f32[24,8208]{1,0:T(8,128)S(1)}, s32[]{:T(128)}, /*index=5*/s32[]...) while((s32[]{:T(128)}, f32[8,8192]{1,0:T(8,128)S(1)}, ...), condition=%wide.region_4.5_spmd.clone, body=%wide.region_3.4_spmd.clone.sunk | while | flops 2162713 | bytes 4721729 | solution.py:93
  97.5 1.4 fusion.159
  99.3 1.4 fusion.159
  101.2 1.4 fusion.159
  103.0 1.4 fusion.159
  104.9 1.4 fusion.159
  106.7 1.4 fusion.159
  108.6 1.4 fusion.159
  110.5 1.4 fusion.159
  112.3 1.4 fusion.159
  116.0 1.4 fusion.159
  117.8 1.4 fusion.159
  119.7 1.4 fusion.159
  121.5 1.4 fusion.159
  127.3 4.3 collective-permute-start.6
  132.9 2.1 collective-permute-done.7
  135.3 27.8 %while.148 = (s32[]{:T(128)}, f32[8,8192]{1,0:T(8,128)S(1)}, f32[8,16,16]{2,0,1:T(8,128)S(1)}, f32[24,8208]{1,0:T(8,128)S(1)}, s32[]{:T(128)}, /*index=5*/s32[]{...) while((s32[]{:T(128)}, f32[8,8192]{1,0:T(8,128)S(1)}, ...), condition=%wide.region_8.9_spmd.clone, body=%wide.region_7.8_spmd.clone.sunk | while | flops 2162706 | bytes 4721599 | solution.py:71
  163.9 42.4 %all-reduce.19 = (f32[]{:T(128)}, f32[]{:T(128)}) all-reduce(f32[]{:T(128)} %get-tuple-element.1221, f32[]{:T(128)} %fusion.137), channel_id=1, replica_groups=mesh['rows'=8,'scales'=4] {'rows','scales'}, use_global_device_ids=true, to_apply=%region_6.7 | all-reduce | flops 2 | bytes 16 | tf_op jit(solution)/shard_map/psum | solution.py:128
  208.5 17.4 %all-gather.4.cloned.1.call-done = f32[32,8192]{1,0:T(8,128)} async-done(((f32[8,8192]{1,0:T(8,128)}), f32[32,8192]{1,0:T(8,128)}) %all-gather.4.cloned.1.call-update) | async-done | bytes 1048592 | tf_op jit(solution)/shard_map/all_gather | solution.py:134
  225.8 4.2 multiply_add_fusion.5
  231.2 2.2 select_select_fusion.3
  233.5 2.3 select_select_fusion.2
  236.8 5.5 all-to-all-start.1
  243.4 25.1 %all-to-all-done.1 = f32[32,8,1024]{2,0,1:T(8,128)S(1)} async-done(((f32[32,8,1024]{2,0,1:T(8,128)}), f32[32,8,1024]{2,0,1:T(8,128)S(1)}, u32[]{:S(2)}, u32[]{:S(2)}) %all-to-all-start.1) | async-done | bytes 1048608 | tf_op jit(solution)/shard_map/all_to_all | solution.py:146
  268.5 3.8 all-to-all-start
  274.4 23.8 %all-to-all-done = f32[32,8,1024]{2,0,1:T(8,128)S(1)} async-done(((f32[32,8,1024]{2,0,1:T(8,128)}), f32[32,8,1024]{2,0,1:T(8,128)S(1)}, u32[]{:S(2)}, u32[]{:S(2)}) %all-to-all-start) | async-done | bytes 1048608 | tf_op jit(solution)/shard_map/all_to_all | solution.py:145
  298.5 30.1 %all_to_all.114 = f32[8,32,1024]{2,1,0:T(8,128)S(1)} all-to-all(f32[8,32,1024]{2,1,0:T(8,128)S(1)} %bitcast.72), channel_id=1, replica_groups=mesh['rows'=8,'scales'=4] {'rows'}, dimensions={0} | all-to-all | bytes 2097152 | tf_op jit(solution)/shard_map/all_to_all | solution.py:156
  329.9 24.7 %reduce-scatter.3.cloned.1.call-done = f32[8,8192]{1,0:T(8,128)} async-done(((f32[32,8192]{1,0:T(8,128)}), f32[8,8192]{1,0:T(8,128)}) %reduce-scatter.3.cloned.1.call-update) | async-done | bytes 262160 | tf_op jit(solution)/shard_map/reduce_scatter | solution.py:157
  355.6 1.6 collective-permute-start.8
  358.5 2.4 collective-permute-done.9
  361.2 27.8 %while.149 = (s32[]{:T(128)}, f32[8,8192]{1,0:T(8,128)S(1)}, f32[8,16,16]{2,0,1:T(8,128)S(1)}, f32[24,8208]{1,0:T(8,128)S(1)}, s32[]{:T(128)}, /*index=5*/s32[]{...) while((s32[]{:T(128)}, f32[8,8192]{1,0:T(8,128)S(1)}, ...), condition=%wide.region_18.19_spmd.clone, body=%wide.region_17.18_spmd.clone.sunk | while | flops 2162706 | bytes 4721599 | solution.py:71
  389.0 6.7 collective-permute-start.10
  395.7 1.5 collective-permute-start.11
  397.2 1.9 collective-permute-done.11
  399.4 29.6 %while.150 = (s32[]{:T(128)}, f32[8,8192]{1,0:T(8,128)S(1)}, f32[24,16,16]{2,0,1:T(8,128)S(1)}, f32[24,8208]{1,0:T(8,128)S(1)}, s32[]{:T(128)}, /*index=5*/s32[]...) while((s32[]{:T(128)}, f32[8,8192]{1,0:T(8,128)S(1)}, ...), condition=%wide.region_20.21_spmd.clone, body=%wide.region_19.20_spmd.clone.sunk | while | flops 2162713 | bytes 4721729 | solution.py:93
  399.9 1.4 fusion.162
  401.7 1.4 fusion.162
  403.6 1.4 fusion.162
  405.4 1.4 fusion.162
  407.3 1.4 fusion.162
  409.1 1.4 fusion.162
  411.0 1.4 fusion.162
  412.8 1.4 fusion.162
  414.7 1.4 fusion.162
  429.6 8.0 %collective-permute-start.12 = (f32[8,8192]{1,0:T(8,128)S(1)}, f32[8,8192]{1,0:T(8,128)S(1)}, u32[]{:S(2)}, u32[]{:S(2)}) collective-permute-start(f32[8,8192]{1,0:T(8,128)S(1)} %get-tuple-element.1218), channel_id=1, source_target_pairs={{0,1},{1,2},{2,3},{3,4},{4,5},{5,6},{6,7},{7,8},{8,9},{9,10},{10,1... | collective-permute-start | bytes 786440 | tf_op jit(solution)/shard_map/ppermute | solution.py:21
  439.0 2.1 collective-permute-done.13
  441.4 27.8 %while.151 = (s32[]{:T(128)}, f32[8,8192]{1,0:T(8,128)S(1)}, f32[8,16,16]{2,0,1:T(8,128)S(1)}, f32[24,8208]{1,0:T(8,128)S(1)}, s32[]{:T(128)}, /*index=5*/s32[]{...) while((s32[]{:T(128)}, f32[8,8192]{1,0:T(8,128)S(1)}, ...), condition=%wide.region_24.25_spmd.clone, body=%wide.region_23.24_spmd.clone.sunk | while | flops 2162706 | bytes 4721599 | solution.py:71
  470.0 47.3 %all-reduce.18 = (f32[]{:T(128)}, f32[]{:T(128)}) all-reduce(f32[]{:T(128)} %get-tuple-element.1217, f32[]{:T(128)} %fusion.138), channel_id=1, replica_groups=mesh['rows'=8,'scales'=4] {'rows','scales'}, use_global_device_ids=true, to_apply=%region_22.23 | all-reduce | flops 2 | bytes 16 | tf_op jit(solution)/shard_map/psum | solution.py:128
  519.4 18.3 %all-gather.6.cloned.1.call-done = f32[32,8192]{1,0:T(8,128)} async-done(((f32[8,8192]{1,0:T(8,128)}), f32[32,8192]{1,0:T(8,128)}) %all-gather.6.cloned.1.call-update) | async-done | bytes 1048592 | tf_op jit(solution)/shard_map/all_gather | solution.py:134
  537.6 4.2 multiply_add_fusion.2
  543.0 2.2 select_select_fusion.1
  545.3 2.2 select_select_fusion
  548.6 5.5 all-to-all-start.4
  555.2 25.1 %all-to-all-done.4 = f32[32,8,1024]{2,0,1:T(8,128)S(1)} async-done(((f32[32,8,1024]{2,0,1:T(8,128)}), f32[32,8,1024]{2,0,1:T(8,128)S(1)}, u32[]{:S(2)}, u32[]{:S(2)}) %all-to-all-start.4) | async-done | bytes 1048608 | tf_op jit(solution)/shard_map/all_to_all | solution.py:146
  580.3 3.6 all-to-all-start.3
  585.4 24.4 %all-to-all-done.3 = f32[32,8,1024]{2,0,1:T(8,128)S(1)} async-done(((f32[32,8,1024]{2,0,1:T(8,128)}), f32[32,8,1024]{2,0,1:T(8,128)S(1)}, u32[]{:S(2)}, u32[]{:S(2)}) %all-to-all-start.3) | async-done | bytes 1048608 | tf_op jit(solution)/shard_map/all_to_all | solution.py:145
  610.2 30.1 %all_to_all.115 = f32[8,32,1024]{2,1,0:T(8,128)S(1)} all-to-all(f32[8,32,1024]{2,1,0:T(8,128)S(1)} %bitcast.71), channel_id=1, replica_groups=mesh['rows'=8,'scales'=4] {'rows'}, dimensions={0} | all-to-all | bytes 2097152 | tf_op jit(solution)/shard_map/all_to_all | solution.py:156
  641.4 24.8 %reduce-scatter.5.cloned.1.call-done = f32[8,8192]{1,0:T(8,128)} async-done(((f32[32,8192]{1,0:T(8,128)}), f32[8,8192]{1,0:T(8,128)}) %reduce-scatter.5.cloned.1.call-update) | async-done | bytes 262160 | tf_op jit(solution)/shard_map/reduce_scatter | solution.py:157
  (351 shorter events, 167.6 us)
Async XLA Ops:
  6.5 219.3 %all-gather.4.cloned.1.call-start = ((), (), s32[]{:S(2)}) async-start(), calls=%async_computation.8 | async-start | bytes 1310720 | tf_op jit(solution)/shard_map/all_gather | solution.py:134
  7.6 50.3 %collective-permute-start.2 = (f32[8,8192]{1,0:T(8,128)S(1)}, f32[8,8192]{1,0:T(8,128)S(1)}, u32[]{:S(2)}, u32[]{:S(2)}) collective-permute-start(f32[8,8192]{1,0:T(8,128)S(1)} %sub.46), channel_id=1, source_target_pairs={{0,1},{1,2},{2,3},{3,4},{4,5},{5,6},{6,7},{7,8},{8,9},{9,10},{10,1... | collective-permute-start | bytes 786440 | tf_op jit(solution)/shard_map/ppermute | solution.py:21
  10.0 47.9 %collective-permute-start.3 = (f32[8,8192]{1,0:T(8,128)S(1)}, f32[8,8192]{1,0:T(8,128)S(1)}, u32[]{:S(2)}, u32[]{:S(2)}) collective-permute-start(f32[8,8192]{1,0:T(8,128)S(1)} %sub.46), channel_id=1, source_target_pairs={{1,0},{2,1},{3,2},{4,3},{5,4},{6,5},{7,6},{8,7},{9,8},{10,9},{11,1... | collective-permute-start | bytes 786440 | tf_op jit(solution)/shard_map/ppermute | solution.py:23
  58.2 27.8 %copy-start = (f32[8,8192]{1,0:T(8,128)S(1)}, f32[8,8192]{1,0:T(8,128)}, u32[]{:S(2)}) copy-start(f32[8,8192]{1,0:T(8,128)} %param.29) | copy-start | bytes 786436
  86.1 10.6 %collective-permute-start.4 = (f32[8,8192]{1,0:T(8,128)S(1)}, f32[8,8192]{1,0:T(8,128)S(1)}, u32[]{:S(2)}, u32[]{:S(2)}) collective-permute-start(f32[8,8192]{1,0:T(8,128)S(1)} %mul.2942), channel_id=1, source_target_pairs={{0,1},{1,2},{2,3},{3,4},{4,5},{5,6},{6,7},{7,8},{8,9},{9,10},{10,1... | collective-permute-start | bytes 786440 | tf_op jit(solution)/shard_map/ppermute | solution.py:21
  88.4 8.4 %collective-permute-start.5 = (f32[8,8192]{1,0:T(8,128)S(1)}, f32[8,8192]{1,0:T(8,128)S(1)}, u32[]{:S(2)}, u32[]{:S(2)}) collective-permute-start(f32[8,8192]{1,0:T(8,128)S(1)} %mul.2942), channel_id=1, source_target_pairs={{1,0},{2,1},{3,2},{4,3},{5,4},{6,5},{7,6},{8,7},{9,8},{10,9},{11,1... | collective-permute-start | bytes 786440 | tf_op jit(solution)/shard_map/ppermute | solution.py:23
  89.7 4.4 collective-permute-start
  92.7 3.8 collective-permute-start.1
  97.0 29.6 %copy-start.5 = (f32[8,8192]{1,0:T(8,128)S(1)}, f32[8,8192]{1,0:T(8,128)}, u32[]{:S(2)}) copy-start(f32[8,8192]{1,0:T(8,128)} %param.28) | copy-start | bytes 786436
  127.3 5.6 collective-permute-start.6
  131.6 3.4 collective-permute-start.7
  135.3 72.4 %copy-start.1 = (f32[8,8192]{1,0:T(8,128)S(1)}, f32[8,8192]{1,0:T(8,128)}, u32[]{:S(2)}) copy-start(f32[8,8192]{1,0:T(8,128)} %param.27) | copy-start | bytes 786436
  230.0 1.2 copy-start.2
  236.8 31.7 %all-to-all-start.1 = ((f32[32,8,1024]{2,0,1:T(8,128)}), f32[32,8,1024]{2,0,1:T(8,128)S(1)}, u32[]{:S(2)}, u32[]{:S(2)}) async-start(f32[32,8,1024]{2,0,1:T(8,128)} %bitcast.50), calls=%async_computation.1 | async-start | bytes 2097152 | tf_op jit(solution)/shard_map/all_to_all | solution.py:146
  268.5 3.8 copy-start.6
  268.5 29.7 %all-to-all-start = ((f32[32,8,1024]{2,0,1:T(8,128)}), f32[32,8,1024]{2,0,1:T(8,128)S(1)}, u32[]{:S(2)}, u32[]{:S(2)}) async-start(f32[32,8,1024]{2,0,1:T(8,128)} %bitcast.68), calls=%async_computation | async-start | bytes 2097152 | tf_op jit(solution)/shard_map/all_to_all | solution.py:145
  272.3 82.3 %reduce-scatter.3.cloned.1.call-start = ((), (), s32[]{:S(2)}) async-start(), calls=%async_computation.9 | async-start | bytes 1310720 | tf_op jit(solution)/shard_map/reduce_scatter | solution.py:157
  329.8 207.8 %all-gather.6.cloned.1.call-start = ((), (), s32[]{:S(2)}) async-start(), calls=%async_computation.10 | async-start | bytes 1310720 | tf_op jit(solution)/shard_map/all_gather | solution.py:134
  355.6 2.9 collective-permute-start.8
  357.2 3.7 collective-permute-start.9
  389.0 8.2 %collective-permute-start.10 = (f32[8,8192]{1,0:T(8,128)S(1)}, f32[8,8192]{1,0:T(8,128)S(1)}, u32[]{:S(2)}, u32[]{:S(2)}) collective-permute-start(f32[8,8192]{1,0:T(8,128)S(1)} %mul.2961), channel_id=1, source_target_pairs={{0,1},{1,2},{2,3},{3,4},{4,5},{5,6},{6,7},{7,8},{8,9},{9,10},{10,1... | collective-permute-start | bytes 786440 | tf_op jit(solution)/shard_map/ppermute | solution.py:21
  395.7 3.4 collective-permute-start.11
  429.6 9.4 %collective-permute-start.12 = (f32[8,8192]{1,0:T(8,128)S(1)}, f32[8,8192]{1,0:T(8,128)S(1)}, u32[]{:S(2)}, u32[]{:S(2)}) collective-permute-start(f32[8,8192]{1,0:T(8,128)S(1)} %get-tuple-element.1218), channel_id=1, source_target_pairs={{0,1},{1,2},{2,3},{3,4},{4,5},{5,6},{6,7},{7,8},{8,9},{9,10},{10,1... | collective-permute-start | bytes 786440 | tf_op jit(solution)/shard_map/ppermute | solution.py:21
  437.7 3.4 collective-permute-start.13
  441.4 77.2 %copy-start.4 = (f32[8,8192]{1,0:T(8,128)S(1)}, f32[8,8192]{1,0:T(8,128)}, u32[]{:S(2)}) copy-start(f32[8,8192]{1,0:T(8,128)} %reduce-scatter.3.cloned.1.call-done) | copy-start | bytes 786436
  541.8 1.2 copy-start.3
  548.6 31.7 %all-to-all-start.4 = ((f32[32,8,1024]{2,0,1:T(8,128)}), f32[32,8,1024]{2,0,1:T(8,128)S(1)}, u32[]{:S(2)}, u32[]{:S(2)}) async-start(f32[32,8,1024]{2,0,1:T(8,128)} %bitcast.48), calls=%async_computation.5 | async-start | bytes 2097152 | tf_op jit(solution)/shard_map/all_to_all | solution.py:146
  580.3 29.6 %all-to-all-start.3 = ((f32[32,8,1024]{2,0,1:T(8,128)}), f32[32,8,1024]{2,0,1:T(8,128)S(1)}, u32[]{:S(2)}, u32[]{:S(2)}) async-start(f32[32,8,1024]{2,0,1:T(8,128)} %bitcast.49), calls=%async_computation.4 | async-start | bytes 2097152 | tf_op jit(solution)/shard_map/all_to_all | solution.py:145
  583.9 82.3 %reduce-scatter.5.cloned.1.call-start = ((), (), s32[]{:S(2)}) async-start(), calls=%async_computation.11 | async-start | bytes 1310720 | tf_op jit(solution)/shard_map/reduce_scatter | solution.py:157
Sparse Core Ops, SparseCore 0:
  208.6 17.2 all-gather.3
  329.9 24.6 reduce-scatter.2
  519.5 18.0 all-gather.5
  641.5 24.6 reduce-scatter.4
where the time goes:
time: 674 us; the launch traced here: 673 us
  blocking collectives  196 us (29%)
  waiting for transfers between devices  195 us (29%)
  other arithmetic  156 us (23%)
  starting transfers between devices  56.1 us (8%)
  local copies, waits for them, and re-layouts  49.5 us (7%)
  between operations  17.6 us (3%)
    psum x2, blocking collectives, body(): lax.psum((jnp.sum(descent * descent), jnp.sum(hessian_weight * blurred *...  89.8 us
    add x64, other arithmetic, forward_add_tap_row(): summed + tap_weights[:, column:column + 1] * shifted[:, column:column + c...  81 us
    all_to_all x2, blocking collectives, body(): lax.all_to_all(kept, 'rows', split_axis=0, concat_axis=1, tiled=True)  60.3 us
    all_to_all x2, waiting for transfers between devices, body(): lax.all_to_all(upper, 'rows', split_axis=1, concat_axis=0, tiled=True)  50.2 us
    reduce_scatter x2, waiting for transfers between devices, body(): lax.psum_scatter(contribution, 'scales', scatter_dimension=0, tiled=True)  49.5 us
    all_to_all x2, waiting for transfers between devices, body(): lax.all_to_all(lower, 'rows', split_axis=1, concat_axis=0, tiled=True)  48.3 us
    all_gather x1, blocking collectives, body(): tiles_in = lax.all_gather(psf_tiles, ('rows', 'scales'), axis=0, tiled=True)  45.4 us
    add x32, other arithmetic, adjoint_add_tap_row(): summed + tap_weights[:, column:column + 1] * shifted[:, offset_col:offset...  43.6 us
  transfers between devices with their start and end apart: 22, of which 13 were waited for; matrix products, arithmetic and copies ran while one was open for 1% of the time, Pallas kernels for 0%

commit v1 on v0

--- a/solution.py
+++ b/solution.py
@@ -131,7 +131,24 @@
         )
         step_size = totals[0] / totals[1]
         trial = current - step_size * descent
-        stripe = lax.all_gather(trial, "scales", axis=0, tiled=True)
+        size, index, rows = (lax.axis_size("scales"), lax.axis_index("scales"), trial.shape[0])
+        right = [(i_2, (i_2 + 1) % size) for i_2 in range(size)]
+        downward = [(i_2, (i_2 - 1) % size) for i_2 in range(size)]
+        out = jnp.zeros((*trial.shape[:0], size * rows, *trial.shape[0 + 1 :]), trial.dtype)
+        out = lax.dynamic_update_slice_in_dim(out, trial, index * rows, axis=0)
+        from_left = from_right = trial
+        half = size // 2
+        for turn in range(1, half + 1):
+            from_left = lax.ppermute(from_left, "scales", right)
+            out = lax.dynamic_update_slice_in_dim(
+                out, from_left, (index - turn) % size * rows, axis=0
+            )
+            if turn < size - half:
+                from_right = lax.ppermute(from_right, "scales", downward)
+                out = lax.dynamic_update_slice_in_dim(
+                    out, from_right, (index + turn) % size * rows, axis=0
+                )
+        stripe = out
         smooth = stripe
         lower = jnp.zeros_like(stripe)
         upper = jnp.zeros_like(stripe)

time: 674 us -> 654 us (0.970)
  waiting for transfers between devices: 195 us -> 172 us
  starting transfers between devices: 56.1 us -> 65.8 us
  other arithmetic: 156 us -> 148 us
    all_gather x2 -> x0, waiting for transfers between devices: 35.6 us -> none  [body(): stripe = lax.all_gather(trial, 'scales', axis=0, tiled=True)]
    ppermute x0 -> x6, waiting for transfers between devices: none -> 14.1 us  [the longest x4 14.1 us: body(): from_left = lax.ppermute(from_left, 'scales', right)]
    ppermute x0 -> x6, starting transfers between devices: none -> 9.03 us  [the longest x4 5.64 us: body(): from_left = lax.ppermute(from_left, 'scales', right)]
  transfers between devices with their start and end apart: 22 -> 26, of which waited for: 13 -> 15; matrix products, arithmetic and copies ran while one was open for 1% -> 1% of each run, Pallas kernels for 0% -> 0%
where the time goes in v1:
time: 654 us; the launch traced here: 652 us
  blocking collectives  195 us (30%)
  waiting for transfers between devices  172 us (26%)
  other arithmetic  148 us (23%)
  starting transfers between devices  65.8 us (10%)
  local copies, waits for them, and re-layouts  49.7 us (8%)
  between operations  18 us (3%)
    psum x2, blocking collectives, body(): lax.psum((jnp.sum(descent * descent), jnp.sum(hessian_weight * blurred *...  89.6 us
    add x64, other arithmetic, forward_add_tap_row(): summed + tap_weights[:, column:column + 1] * shifted[:, column:column + c...  81 us
    all_to_all x2, blocking collectives, body(): lax.all_to_all(kept, 'rows', split_axis=0, concat_axis=1, tiled=True)  60.3 us
    all_to_all x2, waiting for transfers between devices, body(): lax.all_to_all(upper, 'rows', split_axis=1, concat_axis=0, tiled=True)  51.6 us
    all_to_all x2, waiting for transfers between devices, body(): lax.all_to_all(lower, 'rows', split_axis=1, concat_axis=0, tiled=True)  48.8 us
    reduce_scatter x2, waiting for transfers between devices, body(): lax.psum_scatter(contribution, 'scales', scatter_dimension=0, tiled=True)  46.2 us
    all_gather x1, blocking collectives, body(): tiles_in = lax.all_gather(psf_tiles, ('rows', 'scales'), axis=0, tiled=True)  45.4 us
    add x32, other arithmetic, adjoint_add_tap_row(): summed + tap_weights[:, column:column + 1] * shifted[:, offset_col:offset...  43.6 us
  transfers between devices with their start and end apart: 26, of which 15 were waited for; matrix products, arithmetic and copies ran while one was open for 1% of the time, Pallas kernels for 0%

profile of v1, /device:TPU:0, one launch (start us, length us, event | category | flops | bytes accessed | tf_op | source)
XLA Modules:
  0.0 652.4 jit_solution(17945894191161241159)
XLA Ops:
  7.6 2.4 collective-permute-start.2
  12.2 45.4 %all-gather = f32[32,1,256]{2,1,0:T(1,128)S(1)} all-gather(f32[1,1,256]{2,1,0:T(1,128)} %bitcast.79), channel_id=1, replica_groups=mesh['rows'=8,'scales'=4] {'rows','scales'}, dimensions={0}, use_global_device_ids=true | all-gather | bytes 33792 | tf_op jit(solution)/shard_map/all_gather | solution.py:105
  58.2 27.8 %while.146 = (s32[]{:T(128)}, f32[8,8192]{1,0:T(8,128)S(1)}, f32[8,16,16]{2,0,1:T(8,128)S(1)}, f32[24,8208]{1,0:T(8,128)S(1)}, s32[]{:T(128)}, /*index=5*/s32[]{...) while((s32[]{:T(128)}, f32[8,8192]{1,0:T(8,128)S(1)}, ...), condition=%wide.region_2.3_spmd.clone, body=%wide.region_1.2_spmd.clone.sunk | while | flops 2162706 | bytes 4721599 | solution.py:71
  86.1 2.3 collective-permute-start.4
  89.7 3.0 collective-permute-start
  94.0 2.5 collective-permute-done.1
  97.0 29.6 %while.147 = (s32[]{:T(128)}, f32[8,8192]{1,0:T(8,128)S(1)}, f32[24,16,16]{2,0,1:T(8,128)S(1)}, f32[24,8208]{1,0:T(8,128)S(1)}, s32[]{:T(128)}, /*index=5*/s32[]...) while((s32[]{:T(128)}, f32[8,8192]{1,0:T(8,128)S(1)}, ...), condition=%wide.region_4.5_spmd.clone, body=%wide.region_3.4_spmd.clone.sunk | while | flops 2162713 | bytes 4721729 | solution.py:93
  97.5 1.4 fusion.159
  99.3 1.4 fusion.159
  101.2 1.4 fusion.159
  103.0 1.4 fusion.159
  104.9 1.4 fusion.159
  106.7 1.4 fusion.159
  108.6 1.4 fusion.159
  110.4 1.4 fusion.159
  112.3 1.4 fusion.159
  127.3 4.3 collective-permute-start.6
  132.9 2.1 collective-permute-done.7
  135.3 27.8 %while.148 = (s32[]{:T(128)}, f32[8,8192]{1,0:T(8,128)S(1)}, f32[8,16,16]{2,0,1:T(8,128)S(1)}, f32[24,8208]{1,0:T(8,128)S(1)}, s32[]{:T(128)}, /*index=5*/s32[]{...) while((s32[]{:T(128)}, f32[8,8192]{1,0:T(8,128)S(1)}, ...), condition=%wide.region_8.9_spmd.clone, body=%wide.region_7.8_spmd.clone.sunk | while | flops 2162706 | bytes 4721599 | solution.py:71
  163.8 42.3 %all-reduce.19 = (f32[]{:T(128)}, f32[]{:T(128)}) all-reduce(f32[]{:T(128)} %get-tuple-element.1249, f32[]{:T(128)} %fusion.137), channel_id=1, replica_groups=mesh['rows'=8,'scales'=4] {'rows','scales'}, use_global_device_ids=true, to_apply=%region_6.7 | all-reduce | flops 2 | bytes 16 | tf_op jit(solution)/shard_map/psum | solution.py:128
  207.8 1.7 collective-permute-start.9
  209.4 4.1 collective-permute-done.8
  213.5 2.8 collective-permute-start.10
  216.3 3.0 collective-permute-done.10
  221.6 2.3 select_select_fusion.3
  223.9 2.2 select_select_fusion.2
  227.2 5.6 all-to-all-start.1
  233.9 25.9 %all-to-all-done.1 = f32[32,8,1024]{2,0,1:T(8,128)S(1)} async-done(((f32[32,8,1024]{2,0,1:T(8,128)}), f32[32,8,1024]{2,0,1:T(8,128)S(1)}, u32[]{:S(2)}, u32[]{:S(2)}) %all-to-all-start.1) | async-done | bytes 1048608 | tf_op jit(solution)/shard_map/all_to_all | solution.py:163
  259.8 3.8 all-to-all-start
  265.7 23.9 %all-to-all-done = f32[32,8,1024]{2,0,1:T(8,128)S(1)} async-done(((f32[32,8,1024]{2,0,1:T(8,128)}), f32[32,8,1024]{2,0,1:T(8,128)S(1)}, u32[]{:S(2)}, u32[]{:S(2)}) %all-to-all-start) | async-done | bytes 1048608 | tf_op jit(solution)/shard_map/all_to_all | solution.py:162
  289.9 30.1 %all_to_all.114 = f32[8,32,1024]{2,1,0:T(8,128)S(1)} all-to-all(f32[8,32,1024]{2,1,0:T(8,128)S(1)} %bitcast.72), channel_id=1, replica_groups=mesh['rows'=8,'scales'=4] {'rows'}, dimensions={0} | all-to-all | bytes 2097152 | tf_op jit(solution)/shard_map/all_to_all | solution.py:173
  321.2 23.1 %reduce-scatter.3.cloned.1.call-done = f32[8,8192]{1,0:T(8,128)} async-done(((f32[32,8192]{1,0:T(8,128)}), f32[8,8192]{1,0:T(8,128)}) %reduce-scatter.3.cloned.1.call-update) | async-done | bytes 262160 | tf_op jit(solution)/shard_map/reduce_scatter | solution.py:174
  345.3 1.6 collective-permute-start.11
  348.2 2.4 collective-permute-done.12
  350.8 27.8 %while.149 = (s32[]{:T(128)}, f32[8,8192]{1,0:T(8,128)S(1)}, f32[8,16,16]{2,0,1:T(8,128)S(1)}, f32[24,8208]{1,0:T(8,128)S(1)}, s32[]{:T(128)}, /*index=5*/s32[]{...) while((s32[]{:T(128)}, f32[8,8192]{1,0:T(8,128)S(1)}, ...), condition=%wide.region_18.19_spmd.clone, body=%wide.region_17.18_spmd.clone.sunk | while | flops 2162706 | bytes 4721599 | solution.py:71
  378.7 6.7 %collective-permute-start.13 = (f32[8,8192]{1,0:T(8,128)S(1)}, f32[8,8192]{1,0:T(8,128)S(1)}, u32[]{:S(2)}, u32[]{:S(2)}) collective-permute-start(f32[8,8192]{1,0:T(8,128)S(1)} %mul.2981), channel_id=1, source_target_pairs={{0,1},{1,2},{2,3},{3,4},{4,5},{5,6},{6,7},{7,8},{8,9},{9,10},{10,1... | collective-permute-start | bytes 786440 | tf_op jit(solution)/shard_map/ppermute | solution.py:21
  385.4 1.5 collective-permute-start.14
  386.9 1.9 collective-permute-done.14
  389.1 29.6 %while.150 = (s32[]{:T(128)}, f32[8,8192]{1,0:T(8,128)S(1)}, f32[24,16,16]{2,0,1:T(8,128)S(1)}, f32[24,8208]{1,0:T(8,128)S(1)}, s32[]{:T(128)}, /*index=5*/s32[]...) while((s32[]{:T(128)}, f32[8,8192]{1,0:T(8,128)S(1)}, ...), condition=%wide.region_20.21_spmd.clone, body=%wide.region_19.20_spmd.clone.sunk | while | flops 2162713 | bytes 4721729 | solution.py:93
  389.6 1.4 fusion.162
  391.4 1.4 fusion.162
  393.3 1.4 fusion.162
  395.1 1.4 fusion.162
  397.0 1.4 fusion.162
  398.8 1.4 fusion.162
  400.7 1.4 fusion.162
  402.5 1.4 fusion.162
  404.4 1.4 fusion.162
  419.4 8.0 %collective-permute-start.15 = (f32[8,8192]{1,0:T(8,128)S(1)}, f32[8,8192]{1,0:T(8,128)S(1)}, u32[]{:S(2)}, u32[]{:S(2)}) collective-permute-start(f32[8,8192]{1,0:T(8,128)S(1)} %get-tuple-element.1244), channel_id=1, source_target_pairs={{0,1},{1,2},{2,3},{3,4},{4,5},{5,6},{6,7},{7,8},{8,9},{9,10},{10,1... | collective-permute-start | bytes 786440 | tf_op jit(solution)/shard_map/ppermute | solution.py:21
  428.7 2.1 collective-permute-done.16
  431.1 27.8 %while.151 = (s32[]{:T(128)}, f32[8,8192]{1,0:T(8,128)S(1)}, f32[8,16,16]{2,0,1:T(8,128)S(1)}, f32[24,8208]{1,0:T(8,128)S(1)}, s32[]{:T(128)}, /*index=5*/s32[]{...) while((s32[]{:T(128)}, f32[8,8192]{1,0:T(8,128)S(1)}, ...), condition=%wide.region_24.25_spmd.clone, body=%wide.region_23.24_spmd.clone.sunk | while | flops 2162706 | bytes 4721599 | solution.py:71
  459.7 47.4 %all-reduce.18 = (f32[]{:T(128)}, f32[]{:T(128)}) all-reduce(f32[]{:T(128)} %get-tuple-element.1243, f32[]{:T(128)} %fusion.138), channel_id=1, replica_groups=mesh['rows'=8,'scales'=4] {'rows','scales'}, use_global_device_ids=true, to_apply=%region_22.23 | all-reduce | flops 2 | bytes 16 | tf_op jit(solution)/shard_map/psum | solution.py:128
  508.5 1.7 collective-permute-start.18
  510.3 4.1 collective-permute-done.17
  514.3 2.8 collective-permute-start.19
  517.2 3.0 collective-permute-done.19
  522.5 2.2 select_select_fusion.1
  524.7 2.2 select_select_fusion
  528.0 5.8 all-to-all-start.4
  534.9 25.7 %all-to-all-done.4 = f32[32,8,1024]{2,0,1:T(8,128)S(1)} async-done(((f32[32,8,1024]{2,0,1:T(8,128)}), f32[32,8,1024]{2,0,1:T(8,128)S(1)}, u32[]{:S(2)}, u32[]{:S(2)}) %all-to-all-start.4) | async-done | bytes 1048608 | tf_op jit(solution)/shard_map/all_to_all | solution.py:163
  560.6 3.9 all-to-all-start.3
  566.0 24.9 %all-to-all-done.3 = f32[32,8,1024]{2,0,1:T(8,128)S(1)} async-done(((f32[32,8,1024]{2,0,1:T(8,128)}), f32[32,8,1024]{2,0,1:T(8,128)S(1)}, u32[]{:S(2)}, u32[]{:S(2)}) %all-to-all-start.3) | async-done | bytes 1048608 | tf_op jit(solution)/shard_map/all_to_all | solution.py:162
  591.2 30.1 %all_to_all.115 = f32[8,32,1024]{2,1,0:T(8,128)S(1)} all-to-all(f32[8,32,1024]{2,1,0:T(8,128)S(1)} %bitcast.71), channel_id=1, replica_groups=mesh['rows'=8,'scales'=4] {'rows'}, dimensions={0} | all-to-all | bytes 2097152 | tf_op jit(solution)/shard_map/all_to_all | solution.py:173
  622.5 23.1 %reduce-scatter.5.cloned.1.call-done = f32[8,8192]{1,0:T(8,128)} async-done(((f32[32,8192]{1,0:T(8,128)}), f32[8,8192]{1,0:T(8,128)}) %reduce-scatter.5.cloned.1.call-update) | async-done | bytes 262160 | tf_op jit(solution)/shard_map/reduce_scatter | solution.py:174
  (361 shorter events, 174.2 us)
Async XLA Ops:
  7.6 50.3 %collective-permute-start.2 = (f32[8,8192]{1,0:T(8,128)S(1)}, f32[8,8192]{1,0:T(8,128)S(1)}, u32[]{:S(2)}, u32[]{:S(2)}) collective-permute-start(f32[8,8192]{1,0:T(8,128)S(1)} %sub.54), channel_id=1, source_target_pairs={{0,1},{1,2},{2,3},{3,4},{4,5},{5,6},{6,7},{7,8},{8,9},{9,10},{10,1... | collective-permute-start | bytes 786440 | tf_op jit(solution)/shard_map/ppermute | solution.py:21
  10.0 47.9 %collective-permute-start.3 = (f32[8,8192]{1,0:T(8,128)S(1)}, f32[8,8192]{1,0:T(8,128)S(1)}, u32[]{:S(2)}, u32[]{:S(2)}) collective-permute-start(f32[8,8192]{1,0:T(8,128)S(1)} %sub.54), channel_id=1, source_target_pairs={{1,0},{2,1},{3,2},{4,3},{5,4},{6,5},{7,6},{8,7},{9,8},{10,9},{11,1... | collective-permute-start | bytes 786440 | tf_op jit(solution)/shard_map/ppermute | solution.py:23
  58.2 27.8 %copy-start.1 = (f32[8,8192]{1,0:T(8,128)S(1)}, f32[8,8192]{1,0:T(8,128)}, u32[]{:S(2)}) copy-start(f32[8,8192]{1,0:T(8,128)} %param.29) | copy-start | bytes 786436
  86.1 10.6 %collective-permute-start.4 = (f32[8,8192]{1,0:T(8,128)S(1)}, f32[8,8192]{1,0:T(8,128)S(1)}, u32[]{:S(2)}, u32[]{:S(2)}) collective-permute-start(f32[8,8192]{1,0:T(8,128)S(1)} %mul.2958), channel_id=1, source_target_pairs={{0,1},{1,2},{2,3},{3,4},{4,5},{5,6},{6,7},{7,8},{8,9},{9,10},{10,1... | collective-permute-start | bytes 786440 | tf_op jit(solution)/shard_map/ppermute | solution.py:21
  88.4 8.4 %collective-permute-start.5 = (f32[8,8192]{1,0:T(8,128)S(1)}, f32[8,8192]{1,0:T(8,128)S(1)}, u32[]{:S(2)}, u32[]{:S(2)}) collective-permute-start(f32[8,8192]{1,0:T(8,128)S(1)} %mul.2958), channel_id=1, source_target_pairs={{1,0},{2,1},{3,2},{4,3},{5,4},{6,5},{7,6},{8,7},{9,8},{10,9},{11,1... | collective-permute-start | bytes 786440 | tf_op jit(solution)/shard_map/ppermute | solution.py:23
  89.7 4.4 collective-permute-start
  92.7 3.8 collective-permute-start.1
  97.0 29.6 %copy-start.3 = (f32[8,8192]{1,0:T(8,128)S(1)}, f32[8,8192]{1,0:T(8,128)}, u32[]{:S(2)}) copy-start(f32[8,8192]{1,0:T(8,128)} %param.28) | copy-start | bytes 786436
  127.3 5.6 collective-permute-start.6
  131.6 3.4 collective-permute-start.7
  163.1 44.5 %copy-start = (f32[8,8192]{1,0:T(8,128)S(1)}, f32[8,8192]{1,0:T(8,128)}, u32[]{:S(2)}) copy-start(f32[8,8192]{1,0:T(8,128)} %param.27) | copy-start | bytes 786436
  207.6 5.8 collective-permute-start.8
  207.8 8.5 %collective-permute-start.9 = (f32[8,8192]{1,0:T(8,128)S(1)}, f32[8,8192]{1,0:T(8,128)S(1)}, u32[]{:S(2)}, u32[]{:S(2)}) collective-permute-start(f32[8,8192]{1,0:T(8,128)S(1)} %get-tuple-element.1248), channel_id=1, source_target_pairs={{0,3},{1,0},{2,1},{3,2},{4,7},{5,4},{6,5},{7,6},{8,11},{9,8},{10,9... | collective-permute-start | bytes 786440 | tf_op jit(solution)/shard_map/ppermute | solution.py:147
  213.5 5.8 collective-permute-start.10
  227.2 32.6 %all-to-all-start.1 = ((f32[32,8,1024]{2,0,1:T(8,128)}), f32[32,8,1024]{2,0,1:T(8,128)S(1)}, u32[]{:S(2)}, u32[]{:S(2)}) async-start(f32[32,8,1024]{2,0,1:T(8,128)} %bitcast.50), calls=%async_computation.1 | async-start | bytes 2097152 | tf_op jit(solution)/shard_map/all_to_all | solution.py:163
  259.8 3.8 copy-start.4
  259.8 29.8 %all-to-all-start = ((f32[32,8,1024]{2,0,1:T(8,128)}), f32[32,8,1024]{2,0,1:T(8,128)S(1)}, u32[]{:S(2)}, u32[]{:S(2)}) async-start(f32[32,8,1024]{2,0,1:T(8,128)} %bitcast.68), calls=%async_computation | async-start | bytes 2097152 | tf_op jit(solution)/shard_map/all_to_all | solution.py:162
  263.6 80.7 %reduce-scatter.3.cloned.1.call-start = ((), (), s32[]{:S(2)}) async-start(), calls=%async_computation.8 | async-start | bytes 1310720 | tf_op jit(solution)/shard_map/reduce_scatter | solution.py:174
  345.3 2.9 collective-permute-start.11
  346.9 3.7 collective-permute-start.12
  378.7 8.2 %collective-permute-start.13 = (f32[8,8192]{1,0:T(8,128)S(1)}, f32[8,8192]{1,0:T(8,128)S(1)}, u32[]{:S(2)}, u32[]{:S(2)}) collective-permute-start(f32[8,8192]{1,0:T(8,128)S(1)} %mul.2981), channel_id=1, source_target_pairs={{0,1},{1,2},{2,3},{3,4},{4,5},{5,6},{6,7},{7,8},{8,9},{9,10},{10,1... | collective-permute-start | bytes 786440 | tf_op jit(solution)/shard_map/ppermute | solution.py:21
  385.4 3.4 collective-permute-start.14
  419.4 9.3 %collective-permute-start.15 = (f32[8,8192]{1,0:T(8,128)S(1)}, f32[8,8192]{1,0:T(8,128)S(1)}, u32[]{:S(2)}, u32[]{:S(2)}) collective-permute-start(f32[8,8192]{1,0:T(8,128)S(1)} %get-tuple-element.1244), channel_id=1, source_target_pairs={{0,1},{1,2},{2,3},{3,4},{4,5},{5,6},{6,7},{7,8},{8,9},{9,10},{10,1... | collective-permute-start | bytes 786440 | tf_op jit(solution)/shard_map/ppermute | solution.py:21
  427.4 3.4 collective-permute-start.16
  458.9 49.5 %copy-start.2 = (f32[8,8192]{1,0:T(8,128)S(1)}, f32[8,8192]{1,0:T(8,128)}, u32[]{:S(2)}) copy-start(f32[8,8192]{1,0:T(8,128)} %reduce-scatter.3.cloned.1.call-done) | copy-start | bytes 786436
  508.5 5.9 collective-permute-start.17
  508.5 8.6 %collective-permute-start.18 = (f32[8,8192]{1,0:T(8,128)S(1)}, f32[8,8192]{1,0:T(8,128)S(1)}, u32[]{:S(2)}, u32[]{:S(2)}) collective-permute-start(f32[8,8192]{1,0:T(8,128)S(1)} %get-tuple-element.1242), channel_id=1, source_target_pairs={{0,3},{1,0},{2,1},{3,2},{4,7},{5,4},{6,5},{7,6},{8,11},{9,8},{10,9... | collective-permute-start | bytes 786440 | tf_op jit(solution)/shard_map/ppermute | solution.py:147
  514.3 5.8 collective-permute-start.19
  528.0 32.6 %all-to-all-start.4 = ((f32[32,8,1024]{2,0,1:T(8,128)}), f32[32,8,1024]{2,0,1:T(8,128)S(1)}, u32[]{:S(2)}, u32[]{:S(2)}) async-start(f32[32,8,1024]{2,0,1:T(8,128)} %bitcast.48), calls=%async_computation.5 | async-start | bytes 2097152 | tf_op jit(solution)/shard_map/all_to_all | solution.py:163
  560.6 30.3 %all-to-all-start.3 = ((f32[32,8,1024]{2,0,1:T(8,128)}), f32[32,8,1024]{2,0,1:T(8,128)S(1)}, u32[]{:S(2)}, u32[]{:S(2)}) async-start(f32[32,8,1024]{2,0,1:T(8,128)} %bitcast.49), calls=%async_computation.4 | async-start | bytes 2097152 | tf_op jit(solution)/shard_map/all_to_all | solution.py:162
  564.5 81.1 %reduce-scatter.5.cloned.1.call-start = ((), (), s32[]{:S(2)}) async-start(), calls=%async_computation.9 | async-start | bytes 1310720 | tf_op jit(solution)/shard_map/reduce_scatter | solution.py:174
Sparse Core Ops, SparseCore 0:
  321.3 22.9 reduce-scatter.2
  622.6 22.9 reduce-scatter.4
